TPU v7x, 128 devices: a whole 4x4x4 slice. The times are simulated.
128 devices in a mesh: row: 8 (over y, core), col: 16 (over z, x).
Axes of the slice: x: 4, y: 4, z: 4, core: 2. Of those that a mesh axis runs over, the one named last changes fastest.
Arguments:
- amplitudes: float32 [96, 256, 1024], P('col', None, 'row'), may hold values from -6 to 6
- interaction: float32 [16384, 16384], P('row', 'col'), may hold values from -0.5 to 0.5, as said below
- tile_counts: int32 [16], replicated, may hold values from 2 to 6, as said below
- tile_block: int32 [96], replicated, may hold values from -1 to 63, as said below
- recouple_sign: int32 [96], replicated, may hold values from 0 to 1
- orbit_perm: int32 [96, 256], replicated, may hold values from 0 to 255, each once within a row
- particle_energy: float32 [96, 256], P('col'), may hold values from -2 to 2
Outputs:
- sigma: float32 [96, 256, 1024], P('col', None, 'row')
Inputs may be any that keep to these rules, and one draw needn't show every extreme that they name: Owner c holds its live tiles in its first tile_counts[c] slots; the counts sum to 64, and some owner holds 6. `tile_block`: live slots map one to one onto the 64 cross-channel tiles, and slots that are not live hold -1; two live tiles of one owner never lie in the same aligned group of 4 cross-channel tiles. interaction equals its transpose.
All inputs are finite; a program needn't handle non-finite values.
Results may differ from a plain program's by a relative error of at most 0.000061.
Values sent between devices are 32-bit elements; how exact they have to be, the bound alone decides.
A program may use at most 128 MiB of HBM per device.

v0:
```python
import jax
import jax.numpy as jnp
from jax import lax
from jax.sharding import PartitionSpec as P


def split_up(value, dim, length):
    before, after = (value.shape[:dim], value.shape[dim + 1 :])
    return jnp.moveaxis(value.reshape(*before, length, -1, *after), dim, 0)


def sum_at_owner(value, axis, dim):
    length = lax.axis_size(axis)
    tiles = lax.all_to_all(split_up(value, dim, length), axis, 0, 0, tiled=True)
    return jnp.sum(tiles, axis=0)


def tile_recouple(tiles, phases, orders):
    moved = jax.vmap(lambda single, ordering: jnp.take(single, ordering, axis=0))(tiles, orders)
    return moved * phases[:, None, None]


def local(
    amplitudes, interaction, tile_counts, tile_block, recouple_sign, orbit_perm, particle_energy
):
    column_index = lax.axis_index("col")
    row_index = lax.axis_index("row")
    column_count = lax.axis_size("col")
    slots, tile_rows, narrow_cols = amplitudes.shape
    row_blocks = interaction.shape[0] // tile_rows
    col_blocks = interaction.shape[1] // tile_rows
    tile_total = tile_block.shape[0]
    slot_ids = jnp.arange(slots, dtype=jnp.int32)
    is_live = slot_ids < jnp.take(tile_counts, column_index)
    live_mask = is_live.astype(jnp.float32)[:, None, None]
    own_block = jnp.where(
        is_live, lax.dynamic_slice_in_dim(tile_block, column_index * slots, slots), -1
    )
    all_phases = (1 - 2 * recouple_sign).astype(jnp.float32)
    own_phases = lax.dynamic_slice_in_dim(all_phases, column_index * slots, slots)
    own_orders = lax.dynamic_slice_in_dim(orbit_perm, column_index * slots, slots, 0)
    diagonal = particle_energy[:, :, None] * amplitudes
    tile_ids = jnp.arange(tile_total, dtype=jnp.int32)
    peer_ids = jnp.arange(column_count, dtype=jnp.int32)

    def tiles_of(blocks):
        matches = tile_block[None, :] == blocks[:, None]
        return jnp.sum(jnp.where(matches, tile_ids[None, :], 0), axis=1)

    target_col = own_block // col_blocks
    my_blocks = column_index * col_blocks + jnp.arange(col_blocks, dtype=jnp.int32)
    block_tiles = tiles_of(my_blocks)
    widened = lax.all_gather(amplitudes, "row", axis=2, tiled=True)
    widened = tile_recouple(widened, own_phases, own_orders)
    group_blocks = row_index * row_blocks + jnp.arange(row_blocks, dtype=jnp.int32)
    group_tiles = tiles_of(group_blocks)
    is_owned = group_tiles // slots == column_index
    placed = (
        jnp.take(widened, group_tiles % slots, axis=0) * is_owned.astype(jnp.float32)[:, None, None]
    )
    crossed = lax.psum(placed.reshape(row_blocks * tile_rows, widened.shape[2]), "col")
    partial_cols = lax.dot_general(
        interaction,
        crossed,
        (((0,), (0,)), ((), ())),
        precision=lax.Precision.HIGHEST,
        preferred_element_type=jnp.float32,
    )
    own_part = sum_at_owner(partial_cols, "row", 1)
    blocks_here = own_part.reshape(col_blocks, tile_rows, narrow_cols)
    block_inverse = jnp.argsort(jnp.take(orbit_perm, block_tiles, axis=0), axis=1)
    blocks_here = tile_recouple(blocks_here, jnp.take(all_phases, block_tiles), block_inverse)
    block_owner = block_tiles // slots
    choose_mask = block_owner[None, :] == peer_ids[:, None]
    choose_block = jnp.sum(
        jnp.where(choose_mask, jnp.arange(col_blocks, dtype=jnp.int32)[None, :], 0), axis=1
    )
    choose_weight = jnp.max(choose_mask.astype(jnp.float32), axis=1)
    outgoing = jnp.take(blocks_here, choose_block, axis=0) * choose_weight[:, None, None]
    arrived = lax.all_to_all(outgoing, "col", split_axis=0, concat_axis=0, tiled=True)
    returned = jnp.take(arrived, jnp.clip(target_col, 0, column_count - 1), axis=0)
    return (returned + diagonal) * live_mask


def solution(mesh):
    placed = (P("col", None, "row"), P("row", "col"), P(), P(), P(), P(), P("col", None))
    return jax.shard_map(
        local, mesh=mesh, in_specs=placed, out_specs=P("col", None, "row"), check_vma=False
    )
```

profile of v0, /device:TPU:0, one launch (start us, length us, event | category | flops | bytes accessed | tf_op | source)
XLA Modules:
  0.0 393.0 jit_solution(7255663869322990882)
XLA Ops:
  7.4 0.7 all-gather.2.cloned.1.call-update
  8.1 0.0 all-reduce.2.cloned.1.call-start
  8.1 0.7 subtract_convert_fusion
  8.8 0.1 dynamic_slice.11
  8.9 0.7 bitcast_or_fusion
  9.6 0.8 select_reduce_fusion
  10.5 0.1 broadcast_bitcast_fusion
  10.6 0.1 broadcast_in_dim.144
  10.7 0.7 compare_and_fusion
  11.4 45.4 %all-gather.2.cloned.1.call-done = f32[6,256,1024]{2,1,0:T(8,128)} async-done(((f32[6,256,128]{2,1,0:T(8,128)}), f32[6,256,1024]{2,1,0:T(8,128)}) %all-gather.2.cloned.1.call-update) | async-done | bytes 6291472 | tf_op jit(solution)/shard_map/all_gather | solution.py:53
  56.8 30.5 %gather_fusion.5 = f32[1536,1024]{1,0:T(8,128)} fusion(f32[6,256,1024]{2,1,0:T(8,128)} %all-gather.2.cloned.1.call-done, s32[1536]{0:T(1024)S(1)} %reshape.221), kind=kCustom, calls=%fused_computation.5 | custom fusion | bytes 12595200 | tf_op jit(solution)/shard_map/vmap(jit(_take))/gather | solution.py:19
  87.3 4.9 %select_multiply_fusion = f32[6,256,1024]{2,1,0:T(8,128)} fusion(f32[6,256,1024]{2,1,0:T(8,128)} %bitcast.45, f32[6]{0:T(128)S(1)} %dynamic_slice.11, pred[6,256]{1,0:T(8,128)(4,1)S(1)} %compare_and_fusion), kind=kLoop, calls=%fused_computation.9 | loop fusion | flops 3145728 | bytes 12584472 | tf_op jit(solution)/shard_map/mul | solution.py:20
  92.2 7.1 %gather_fusion.1 = f32[8,256,1024]{2,1,0:T(8,128)} fusion(f32[6,256,1024]{2,1,0:T(8,128)} %select_multiply_fusion, s32[1024]{0:T(1024)S(1)} %pad_clamp_fusion.2), kind=kCustom, calls=%fused_computation.1 | custom fusion | bytes 16777248 | tf_op jit(solution)/shard_map/jit(_take)/gather | solution.py:59
  99.3 5.8 %fusion = f32[2048,1024]{1,0:T(8,128)} fusion(f32[8,256,1024]{2,1,0:T(8,128)} %gather_fusion.1, f32[2048]{0:T(1024)S(1)} %bitcast.48, pred[2048]{0:T(1024)(128)(4,1)S(1)} %broadcast_in_dim.145), kind=kLoop, calls=%fused_computation.8 | loop fusion | flops 4194304 | bytes 16787456 | tf_op jit(solution)/shard_map/mul | solution.py:59
  105.1 0.0 all-reduce.2.cloned.1.call-update
  105.1 142.9 %all-reduce.2.cloned.1.call-done = f32[2048,1024]{1,0:T(8,128)} async-done(((f32[2048,1024]{1,0:T(8,128)}), f32[2048,1024]{1,0:T(8,128)}) %all-reduce.2.cloned.1.call-update) | async-done | bytes 8388624 | tf_op jit(solution)/shard_map/psum | solution.py:61
  248.1 31.6 %fusion.5 = f32[1024,1024]{1,0:T(8,128)} fusion(f32[2048,1024]{1,0:T(8,128)} %all-reduce.2.cloned.1.call-done, f32[2048,1024]{1,0:T(8,128)} %param.8), kind=kOutput, calls=%fused_computation.61 | convolution fusion | flops 25769803776 | bytes 20971520 | tf_op jit(solution)/shard_map/dot_general | solution.py:62
  279.7 4.7 %all-to-all-start = ((f32[8,1024,128]{1,2,0:T(8,128)}), f32[8,1024,128]{1,2,0:T(8,128)}, u32[]{:S(2)}, u32[]{:S(2)}) async-start(f32[8,1024,128]{1,2,0:T(8,128)} %bitcast.46), calls=%async_computation | async-start | bytes 8388608 | tf_op jit(solution)/shard_map/all_to_all | solution.py:14
  284.4 0.2 sort.19.cloned.1.call-start
  284.6 0.2 select_reduce_fusion.2
  284.8 0.6 gather_fusion.2
  285.5 1.5 gather_fusion
  286.9 0.7 broadcast_select_fusion
  287.6 0.6 iota.37
  288.2 0.0 sort.19.cloned.1.call-update
  288.2 0.1 select_reduce_fusion.1
  288.3 0.1 convert_reduce_fusion
  288.4 2.7 sort.19.cloned.1.call-done
  291.1 0.7 fusion.1
  291.8 0.7 compare_and_fusion.1
  292.5 41.5 %all-to-all-done = f32[8,1024,128]{1,2,0:T(8,128)} async-done(((f32[8,1024,128]{1,2,0:T(8,128)}), f32[8,1024,128]{1,2,0:T(8,128)}, u32[]{:S(2)}, u32[]{:S(2)}) %all-to-all-start) | async-done | bytes 4194336 | tf_op jit(solution)/shard_map/all_to_all | solution.py:14
  334.0 2.6 reduce_sum.44
  336.6 0.2 copy.9
  336.8 6.8 %gather_fusion.6 = f32[1024,128]{1,0:T(8,128)S(1)} fusion(f32[4,256,128]{2,1,0:T(8,128)S(1)} %bitcast.44, s32[1024]{0:T(1024)S(1)} %bitcast.43), kind=kCustom, calls=%fused_computation.6 | custom fusion | bytes 1056768 | tf_op jit(solution)/shard_map/vmap(jit(_take))/gather | solution.py:19
  343.6 0.2 select_multiply_fusion.2
  343.8 0.0 copy-start.3
  343.9 0.0 copy-start
  343.9 0.0 copy-start.1
  343.9 0.7 gather_fusion.3
  344.6 1.6 select_multiply_fusion.1
  346.2 4.5 %all-to-all-start.1 = ((f32[16,256,128]{2,1,0:T(8,128)}), f32[16,256,128]{2,1,0:T(8,128)S(1)}, u32[]{:S(2)}, u32[]{:S(2)}) async-start(f32[16,256,128]{2,1,0:T(8,128)} %select_multiply_fusion.1), calls=%async_computation.1 | async-start | bytes 4194304 | tf_op jit(solution)/shard_map/all_to_all | solution.py:80
  350.8 0.0 copy-done.3
  350.8 0.6 dynamic-slice.2
  352.0 0.1 compare_and_fusion.5
  352.1 29.7 %all-to-all-done.1 = f32[16,256,128]{2,1,0:T(8,128)S(1)} async-done(((f32[16,256,128]{2,1,0:T(8,128)}), f32[16,256,128]{2,1,0:T(8,128)S(1)}, u32[]{:S(2)}, u32[]{:S(2)}) %all-to-all-start.1) | async-done | bytes 2097184 | tf_op jit(solution)/shard_map/all_to_all | solution.py:80
  381.8 1.5 gather_fusion.4
  383.2 0.0 copy-done.1
  383.2 2.3 add_multiply_fusion
  (21 shorter events, 0.1 us)
Async XLA Ops:
  7.4 49.4 %all-gather.2.cloned.1.call-start = ((), (), s32[]{:S(2)}) async-start(), calls=%async_computation.2 | async-start | bytes 7077888 | tf_op jit(solution)/shard_map/all_gather | solution.py:53
  8.1 240.0 %all-reduce.2.cloned.1.call-start = ((), (), s32[]{:S(2)}) async-start(), calls=%async_computation.3 | async-start | bytes 16777216 | tf_op jit(solution)/shard_map/psum | solution.py:61
  279.7 4.9 %copy-start.2 = (s32[96]{0:T(128)S(1)}, s32[96]{0:T(128)}, u32[]{:S(2)}) copy-start(s32[96]{0:T(128)} %param.10) | copy-start | bytes 1156
  279.7 54.3 %all-to-all-start = ((f32[8,1024,128]{1,2,0:T(8,128)}), f32[8,1024,128]{1,2,0:T(8,128)}, u32[]{:S(2)}, u32[]{:S(2)}) async-start(f32[8,1024,128]{1,2,0:T(8,128)} %bitcast.46), calls=%async_computation | async-start | bytes 8388608 | tf_op jit(solution)/shard_map/all_to_all | solution.py:14
  284.4 6.7 %sort.19.cloned.1.call-start = ((), (), s32[]{:S(2)}) async-start(), calls=%async_computation.4 | async-start | bytes 24608 | tf_op jit(solution)/shard_map/jit(argsort)/sort | solution.py:71
  343.8 6.9 %copy-start.3 = (s32[16]{0:T(128)S(1)}, s32[16]{0:T(128)}, u32[]{:S(2)}) copy-start(s32[16]{0:T(128)} %param.9) | copy-start | bytes 196
  343.9 39.4 %copy-start = (f32[6,256,128]{2,1,0:T(8,128)S(1)}, f32[6,256,128]{2,1,0:T(8,128)}, u32[]{:S(2)}) copy-start(f32[6,256,128]{2,1,0:T(8,128)} %param.7) | copy-start | bytes 2359300
  343.9 39.4 %copy-start.1 = (f32[6,256]{1,0:T(8,128)S(1)}, f32[6,256]{1,0:T(8,128)}, u32[]{:S(2)}) copy-start(f32[6,256]{1,0:T(8,128)} %param.13) | copy-start | bytes 18436
  346.2 35.5 %all-to-all-start.1 = ((f32[16,256,128]{2,1,0:T(8,128)}), f32[16,256,128]{2,1,0:T(8,128)S(1)}, u32[]{:S(2)}, u32[]{:S(2)}) async-start(f32[16,256,128]{2,1,0:T(8,128)} %select_multiply_fusion.1), calls=%async_computation.1 | async-start | bytes 4194304 | tf_op jit(solution)/shard_map/all_to_all | solution.py:80
Sparse Core Ops, SparseCore 0:
  9.8 46.9 all-gather.1
  105.3 142.7 all-reduce.1
Sparse Core Ops, SparseCore 1:
  288.3 2.5 sort.21.cloned.1.call-done
  (1 shorter events, 0.0 us)
where the time goes:
time: 394 us; the launch traced here: 393 us
  waiting for transfers between devices  260 us (66%)
  local copies, waits for them, and re-layouts  53.2 us (14%)
  matrix products  31.6 us (8%)
  other arithmetic  23.1 us (6%)
  between operations  15.6 us (4%)
  starting transfers between devices  9.24 us (2%)
    psum x1, waiting for transfers between devices, local(): lax.psum(placed.reshape(row_blocks * tile_rows, widened.shape[2]), 'col')  143 us
    all_gather x1, waiting for transfers between devices, local(): widened = lax.all_gather(amplitudes, 'row', axis=2, tiled=True)  45.4 us
    all_to_all x1, waiting for transfers between devices, sum_at_owner(): tiles = lax.all_to_all(split_up(value, dim, length), axis, 0, 0, tiled=True)  41.5 us
    gather x3, local copies, waits for them, and re-layouts, tile_recouple(): jnp.take(single, ordering, axis=0)  37.3 us
    dot_general x1, matrix products, local(): lax.dot_general(interaction, crossed, (((0,), (0,)), ((), ())), precision...  31.6 us
    all_to_all x1, waiting for transfers between devices, local(): lax.all_to_all(outgoing, 'col', split_axis=0, concat_axis=0, tiled=True)  29.7 us
  transfers between devices with their start and end apart: 4, of which 4 were waited for; matrix products, arithmetic and copies ran while one was open for 2% of the time, Pallas kernels for 0%

commit v1 on v0

--- a/solution.py
+++ b/solution.py
@@ -50,7 +50,8 @@
     target_col = own_block // col_blocks
     my_blocks = column_index * col_blocks + jnp.arange(col_blocks, dtype=jnp.int32)
     block_tiles = tiles_of(my_blocks)
-    widened = lax.all_gather(amplitudes, "row", axis=2, tiled=True)
+    sent = jnp.stack([amplitudes] * lax.axis_size("row"))
+    widened = jnp.concatenate(lax.all_to_all(sent, "row", 0, 0), axis=2)
     widened = tile_recouple(widened, own_phases, own_orders)
     group_blocks = row_index * row_blocks + jnp.arange(row_blocks, dtype=jnp.int32)
     group_tiles = tiles_of(group_blocks)

time: 394 us -> 432 us (1.096)
  waiting for transfers between devices: 260 us -> 286 us
  local copies, waits for them, and re-layouts: 53.2 us -> 63.2 us
  starting transfers between devices: 9.24 us -> 14 us
    all_to_all x0 -> x1, waiting for transfers between devices: none -> 71.5 us  [local(): widened = jnp.concatenate(lax.all_to_all(sent, 'row', 0, 0), axis=2)]
    all_gather x1 -> x0, waiting for transfers between devices: 45.4 us -> none  [local(): widened = lax.all_gather(amplitudes, 'row', axis=2, tiled=True)]
    reshape x0 -> x1, local copies, waits for them, and re-layouts: none -> 6.34 us  [local(): widened = jnp.concatenate(lax.all_to_all(sent, 'row', 0, 0), axis=2)]
    all_to_all x0 -> x1, starting transfers between devices: none -> 4.88 us  [local(): widened = jnp.concatenate(lax.all_to_all(sent, 'row', 0, 0), axis=2)]
    another operation x0 -> x1, local copies, waits for them, and re-layouts: none -> 4.54 us  [local(): sent = jnp.stack([amplitudes] * lax.axis_size('row'))]
  transfers between devices with their start and end apart: 4 -> 4, of which waited for: 4 -> 4; matrix products, arithmetic and copies ran while one was open for 2% -> 1% of each run, Pallas kernels for 0% -> 0%
where the time goes in v1:
time: 432 us; the launch traced here: 431 us
  waiting for transfers between devices  286 us (66%)
  local copies, waits for them, and re-layouts  63.2 us (15%)
  matrix products  31.6 us (7%)
  other arithmetic  20.3 us (5%)
  between operations  15.7 us (4%)
  starting transfers between devices  14 us (3%)
    psum x1, waiting for transfers between devices, local(): lax.psum(placed.reshape(row_blocks * tile_rows, widened.shape[2]), 'col')  143 us
    all_to_all x1, waiting for transfers between devices, local(): widened = jnp.concatenate(lax.all_to_all(sent, 'row', 0, 0), axis=2)  71.5 us
    all_to_all x1, waiting for transfers between devices, sum_at_owner(): tiles = lax.all_to_all(split_up(value, dim, length), axis, 0, 0, tiled=True)  42.4 us
    gather x3, local copies, waits for them, and re-layouts, tile_recouple(): jnp.take(single, ordering, axis=0)  37.2 us
    dot_general x1, matrix products, local(): lax.dot_general(interaction, crossed, (((0,), (0,)), ((), ())), precision...  31.6 us
    all_to_all x1, waiting for transfers between devices, local(): lax.all_to_all(outgoing, 'col', split_axis=0, concat_axis=0, tiled=True)  29.7 us
  transfers between devices with their start and end apart: 4, of which 4 were waited for; matrix products, arithmetic and copies ran while one was open for 1% of the time, Pallas kernels for 0%

profile of v1, /device:TPU:0, one launch (start us, length us, event | category | flops | bytes accessed | tf_op | source)
XLA Modules:
  0.0 430.9 jit_solution(17521381890615685139)
XLA Ops:
  7.4 4.5 %stack.2 = f32[8,6,256,128]{3,2,1,0:T(8,128)} broadcast(f32[6,256,128]{2,1,0:T(8,128)} %param.7), dimensions={1,2,3} | broadcast | bytes 7077888 | tf_op jit(solution)/shard_map/stack | solution.py:53
  11.9 4.9 %all-to-all-start = ((f32[8,6,256,128]{3,2,1,0:T(8,128)}), f32[8,6,256,128]{3,2,1,0:T(8,128)}, u32[]{:S(2)}, u32[]{:S(2)}) async-start(f32[8,6,256,128]{3,2,1,0:T(8,128)} %stack.2), calls=%async_computation | async-start | bytes 12582912 | tf_op jit(solution)/shard_map/all_to_all | solution.py:54
  16.8 0.0 all-reduce.2.cloned.1.call-start
  16.9 0.0 copy-done.4
  16.9 0.1 dynamic_slice.11
  17.0 0.0 copy-done.1
  17.0 0.0 copy-done.3
  17.0 0.2 select_reduce_fusion
  17.2 0.1 broadcast_bitcast_fusion
  17.3 0.1 broadcast_in_dim.144
  17.4 71.5 %all-to-all-done = f32[8,6,256,128]{3,2,1,0:T(8,128)} async-done(((f32[8,6,256,128]{3,2,1,0:T(8,128)}), f32[8,6,256,128]{3,2,1,0:T(8,128)}, u32[]{:S(2)}, u32[]{:S(2)}) %all-to-all-start) | async-done | bytes 6291488 | tf_op jit(solution)/shard_map/all_to_all | solution.py:54
  88.9 6.3 %copy_bitcast_fusion = f32[6,256,1024]{2,1,0:T(8,128)} fusion(f32[8,6,256,128]{3,2,1,0:T(8,128)} %all-to-all-done), kind=kLoop, calls=%fused_computation.9 | loop fusion | bytes 12582912 | tf_op jit(solution)/shard_map/reshape | solution.py:54
  95.3 30.4 %gather_fusion.5 = f32[1536,1024]{1,0:T(8,128)} fusion(f32[6,256,1024]{2,1,0:T(8,128)} %copy_bitcast_fusion, s32[1536]{0:T(1024)S(1)} %reshape.231), kind=kCustom, calls=%fused_computation.5 | custom fusion | bytes 12595200 | tf_op jit(solution)/shard_map/vmap(jit(_take))/gather | solution.py:19
  125.7 4.9 %select_multiply_fusion = f32[6,256,1024]{2,1,0:T(8,128)} fusion(f32[6,256,1024]{2,1,0:T(8,128)} %bitcast.51, f32[6]{0:T(128)S(1)} %dynamic_slice.11, pred[6,256]{1,0:T(8,128)(4,1)S(1)} %compare_and_fusion), kind=kLoop, calls=%fused_computation.10 | loop fusion | flops 3145728 | bytes 12584472 | tf_op jit(solution)/shard_map/mul | solution.py:20
  130.6 7.1 %gather_fusion.1 = f32[8,256,1024]{2,1,0:T(8,128)} fusion(f32[6,256,1024]{2,1,0:T(8,128)} %select_multiply_fusion, s32[1024]{0:T(1024)S(1)} %pad_clamp_fusion.2), kind=kCustom, calls=%fused_computation.1 | custom fusion | bytes 16777248 | tf_op jit(solution)/shard_map/jit(_take)/gather | solution.py:60
  137.7 5.8 %fusion = f32[2048,1024]{1,0:T(8,128)} fusion(f32[8,256,1024]{2,1,0:T(8,128)} %gather_fusion.1, f32[2048]{0:T(1024)S(1)} %bitcast.54, pred[2048]{0:T(1024)(128)(4,1)S(1)} %broadcast_in_dim.145), kind=kLoop, calls=%fused_computation.8 | loop fusion | flops 4194304 | bytes 16787456 | tf_op jit(solution)/shard_map/mul | solution.py:60
  143.5 0.0 all-reduce.2.cloned.1.call-update
  143.5 142.6 %all-reduce.2.cloned.1.call-done = f32[2048,1024]{1,0:T(8,128)} async-done(((f32[2048,1024]{1,0:T(8,128)}), f32[2048,1024]{1,0:T(8,128)}) %all-reduce.2.cloned.1.call-update) | async-done | bytes 8388624 | tf_op jit(solution)/shard_map/psum | solution.py:62
  286.1 31.6 %fusion.5 = f32[1024,1024]{1,0:T(8,128)} fusion(f32[2048,1024]{1,0:T(8,128)} %all-reduce.2.cloned.1.call-done, f32[2048,1024]{1,0:T(8,128)} %param.8), kind=kOutput, calls=%fused_computation.62 | convolution fusion | flops 25769803776 | bytes 20971520 | tf_op jit(solution)/shard_map/dot_general | solution.py:63
  317.7 4.5 %all-to-all-start.1 = ((f32[8,1024,128]{1,2,0:T(8,128)}), f32[8,1024,128]{1,2,0:T(8,128)}, u32[]{:S(2)}, u32[]{:S(2)}) async-start(f32[8,1024,128]{1,2,0:T(8,128)} %bitcast.52), calls=%async_computation.1 | async-start | bytes 8388608 | tf_op jit(solution)/shard_map/all_to_all | solution.py:14
  322.3 0.2 sort.19.cloned.1.call-start
  322.5 0.2 select_reduce_fusion.2
  322.7 0.6 gather_fusion.2
  323.4 0.6 gather_fusion
  323.9 0.7 broadcast_select_fusion
  324.6 0.6 iota.37
  325.2 0.0 sort.19.cloned.1.call-update
  325.2 0.1 select_reduce_fusion.1
  325.3 0.1 convert_reduce_fusion
  325.4 2.7 sort.19.cloned.1.call-done
  328.1 0.7 fusion.1
  328.8 0.7 compare_and_fusion.1
  329.5 42.4 %all-to-all-done.1 = f32[8,1024,128]{1,2,0:T(8,128)} async-done(((f32[8,1024,128]{1,2,0:T(8,128)}), f32[8,1024,128]{1,2,0:T(8,128)}, u32[]{:S(2)}, u32[]{:S(2)}) %all-to-all-start.1) | async-done | bytes 4194336 | tf_op jit(solution)/shard_map/all_to_all | solution.py:14
  371.9 2.6 reduce_sum.44
  374.5 0.2 copy.11
  374.7 6.8 %gather_fusion.6 = f32[1024,128]{1,0:T(8,128)S(1)} fusion(f32[4,256,128]{2,1,0:T(8,128)S(1)} %bitcast.50, s32[1024]{0:T(1024)S(1)} %bitcast.49), kind=kCustom, calls=%fused_computation.6 | custom fusion | bytes 1056768 | tf_op jit(solution)/shard_map/vmap(jit(_take))/gather | solution.py:19
  381.5 0.2 select_multiply_fusion.2
  381.7 0.0 copy-start.5
  381.8 0.0 copy-start
  381.8 0.0 copy-start.2
  381.8 0.7 gather_fusion.3
  382.5 1.6 select_multiply_fusion.1
  384.1 4.5 %all-to-all-start.2 = ((f32[16,256,128]{2,1,0:T(8,128)}), f32[16,256,128]{2,1,0:T(8,128)S(1)}, u32[]{:S(2)}, u32[]{:S(2)}) async-start(f32[16,256,128]{2,1,0:T(8,128)} %select_multiply_fusion.1), calls=%async_computation.2 | async-start | bytes 4194304 | tf_op jit(solution)/shard_map/all_to_all | solution.py:81
  388.7 0.6 dynamic-slice.2
  389.9 0.1 compare_and_fusion.5
  390.0 29.7 %all-to-all-done.2 = f32[16,256,128]{2,1,0:T(8,128)S(1)} async-done(((f32[16,256,128]{2,1,0:T(8,128)}), f32[16,256,128]{2,1,0:T(8,128)S(1)}, u32[]{:S(2)}, u32[]{:S(2)}) %all-to-all-start.2) | async-done | bytes 2097184 | tf_op jit(solution)/shard_map/all_to_all | solution.py:81
  419.7 1.5 gather_fusion.4
  421.1 2.3 add_multiply_fusion
  (26 shorter events, 0.2 us)
Async XLA Ops:
  11.9 4.9 %copy-start.4 = (s32[96]{0:T(128)S(1)}, s32[96]{0:T(128)}, u32[]{:S(2)}) copy-start(s32[96]{0:T(128)} %param.11) | copy-start | bytes 1156
  11.9 5.0 %copy-start.1 = (s32[96,256]{1,0:T(8,128)S(1)}, s32[96,256]{1,0:T(8,128)}, u32[]{:S(2)}) copy-start(s32[96,256]{1,0:T(8,128)} %param.12) | copy-start | bytes 294916
  11.9 5.1 %copy-start.3 = (s32[96]{0:T(128)S(1)}, s32[96]{0:T(128)}, u32[]{:S(2)}) copy-start(s32[96]{0:T(128)} %param.10) | copy-start | bytes 1156
  11.9 77.0 %all-to-all-start = ((f32[8,6,256,128]{3,2,1,0:T(8,128)}), f32[8,6,256,128]{3,2,1,0:T(8,128)}, u32[]{:S(2)}, u32[]{:S(2)}) async-start(f32[8,6,256,128]{3,2,1,0:T(8,128)} %stack.2), calls=%async_computation | async-start | bytes 12582912 | tf_op jit(solution)/shard_map/all_to_all | solution.py:54
  16.8 269.3 %all-reduce.2.cloned.1.call-start = ((), (), s32[]{:S(2)}) async-start(), calls=%async_computation.3 | async-start | bytes 16777216 | tf_op jit(solution)/shard_map/psum | solution.py:62
  317.7 54.2 %all-to-all-start.1 = ((f32[8,1024,128]{1,2,0:T(8,128)}), f32[8,1024,128]{1,2,0:T(8,128)}, u32[]{:S(2)}, u32[]{:S(2)}) async-start(f32[8,1024,128]{1,2,0:T(8,128)} %bitcast.52), calls=%async_computation.1 | async-start | bytes 8388608 | tf_op jit(solution)/shard_map/all_to_all | solution.py:14
  322.3 5.9 %sort.19.cloned.1.call-start = ((), (), s32[]{:S(2)}) async-start(), calls=%async_computation.4 | async-start | bytes 24608 | tf_op jit(solution)/shard_map/jit(argsort)/sort | solution.py:72
  381.7 6.9 %copy-start.5 = (s32[16]{0:T(128)S(1)}, s32[16]{0:T(128)}, u32[]{:S(2)}) copy-start(s32[16]{0:T(128)} %param.9) | copy-start | bytes 196
  381.8 39.4 %copy-start = (f32[6,256,128]{2,1,0:T(8,128)S(1)}, f32[6,256,128]{2,1,0:T(8,128)}, u32[]{:S(2)}) copy-start(f32[6,256,128]{2,1,0:T(8,128)} %param.7) | copy-start | bytes 2359300
  381.8 39.4 %copy-start.2 = (f32[6,256]{1,0:T(8,128)S(1)}, f32[6,256]{1,0:T(8,128)}, u32[]{:S(2)}) copy-start(f32[6,256]{1,0:T(8,128)} %param.13) | copy-start | bytes 18436
  384.1 35.5 %all-to-all-start.2 = ((f32[16,256,128]{2,1,0:T(8,128)}), f32[16,256,128]{2,1,0:T(8,128)S(1)}, u32[]{:S(2)}, u32[]{:S(2)}) async-start(f32[16,256,128]{2,1,0:T(8,128)} %select_multiply_fusion.1), calls=%async_computation.2 | async-start | bytes 4194304 | tf_op jit(solution)/shard_map/all_to_all | solution.py:81
Sparse Core Ops, SparseCore 0:
  143.6 142.3 all-reduce.1
Sparse Core Ops, SparseCore 1:
  325.3 2.5 sort.21.cloned.1.call-done
  (1 shorter events, 0.0 us)
